TPU v7x, 512 devices: a whole 4x8x8 slice. The times are simulated.
512 devices in a mesh: dp: 16 (over x, z_hi), tm: 32 (over z_lo, y, core).
Axes of the slice: x: 4, y: 8, z: 8 (z_hi: 4, z_lo: 2; z = z_hi * 2 + z_lo), core: 2. Of those that a mesh axis runs over, the one named last changes fastest.
Arguments:
- activations: bfloat16 [16, 64, 64, 16, 128], P('dp', 'tm')
- conv_weight: bfloat16 [3, 3, 3, 128, 128], replicated, may hold values from -0.109375 to 0.109375
- norm_gain: float32 [128], replicated, may hold values from 0.5 to 1.5
- norm_bias: float32 [128], replicated, may hold values from -0.5 to 0.5
- down_weight: bfloat16 [3, 3, 128, 128], replicated, may hold values from -0.1875 to 0.1875
- cotangent: bfloat16 [16, 64, 32, 8, 128], P('dp', None, 'tm'), may hold values from -0.21875 to 0.21875
Outputs:
- encoded: bfloat16 [16, 64, 32, 8, 128], P('dp', None, 'tm')
- grad_down: float32 [3, 3, 128, 128], P(None, None, None, 'tm')
All inputs are finite; a program needn't handle non-finite values.
Results may differ from a plain program's by a relative error of at most 0.005.
Values may be sent and summed in bfloat16 or wider, within the bound.
A program may use at most 64 MiB of HBM per device.

v0:
```python
import jax
import jax.numpy as jnp
from jax import lax
from jax.sharding import PartitionSpec as P

G = 32


def passed_along(shard, axis, by):
    count = lax.axis_size(axis)
    pairs = [(i, i + by) for i in range(count) if 0 <= i + by < count]
    return lax.ppermute(shard, axis, pairs)


def down_patches(extended, rows_out, cols_out):
    tap_list = []
    for row_tap in range(3):
        for col_tap in range(3):
            tap_list.append(
                extended[
                    :,
                    :,
                    row_tap : row_tap + 2 * rows_out - 1 : 2,
                    col_tap : col_tap + 2 * cols_out - 1 : 2,
                    :,
                ]
            )
    return jnp.concatenate(tap_list, axis=-1)


def per_device(activations, conv_weight, norm_gain, norm_bias, down_weight, cotangent):
    clip_count, frames_dev, height, width_cells, channels = activations.shape
    out_channels = conv_weight.shape[-1]
    groups = G
    earlier = passed_along(activations, "tm", 1)
    framed = jnp.concatenate([earlier, activations], axis=1)
    framed = jnp.pad(framed, ((0, 0), (0, 0), (1, 1), (1, 1), (0, 0)))
    conv_out = jnp.zeros(
        (clip_count * frames_dev * height * width_cells, out_channels), jnp.float32
    )
    for row_tap in range(3):
        for col_tap in range(3):
            window_slab = framed[
                :, :, row_tap : row_tap + height, col_tap : col_tap + width_cells, :
            ]
            stacked = jnp.concatenate(
                [window_slab[:, time_tap : time_tap + frames_dev] for time_tap in range(3)], axis=-1
            )
            tap_weight = conv_weight[:, row_tap, col_tap].reshape(3 * channels, out_channels)
            conv_out = conv_out + jnp.dot(
                stacked.reshape(-1, 3 * channels), tap_weight, preferred_element_type=jnp.float32
            )
    grouped = conv_out.reshape(
        clip_count, frames_dev, height, width_cells, groups, channels // groups
    )
    group_sums = jnp.sum(grouped, axis=(1, 2, 3, 5))
    group_squares = jnp.sum(grouped * grouped, axis=(1, 2, 3, 5))
    group_sums, group_squares = lax.psum((group_sums, group_squares), "tm")
    members = float(frames_dev * lax.axis_size("tm") * height * width_cells * (channels // groups))
    group_mean = group_sums / members
    variance = group_squares / members - group_mean * group_mean
    inverse = lax.rsqrt(variance + 1e-06)
    normed = (
        (grouped - group_mean[:, None, None, None, :, None]) * inverse[:, None, None, None, :, None]
    ).reshape(clip_count, frames_dev, height, width_cells, channels) * norm_gain + norm_bias
    hidden = jax.nn.silu(normed).astype(jnp.bfloat16)
    down_flat = down_weight.reshape(9 * channels, -1)
    row_local = lax.all_to_all(hidden, "tm", split_axis=2, concat_axis=1, tiled=True)
    lower_row = passed_along(row_local[:, :, :1], "tm", -1)
    extended = jnp.concatenate([row_local, lower_row], axis=2)
    extended = jnp.pad(extended, ((0, 0), (0, 0), (0, 0), (0, 1), (0, 0)))
    patches = down_patches(extended, row_local.shape[2] // 2, width_cells // 2)
    encoded = (
        jnp.dot(patches.reshape(-1, 9 * channels), down_flat, preferred_element_type=jnp.float32)
        .reshape(cotangent.shape)
        .astype(jnp.bfloat16)
    )
    partial_value = lax.dot_general(
        patches.reshape(-1, 9 * channels),
        cotangent.reshape(-1, cotangent.shape[-1]),
        (((0,), (0,)), ((), ())),
        preferred_element_type=jnp.float32,
    )
    partial_value = partial_value.reshape(3, 3, channels, -1)
    shares = lax.psum_scatter(partial_value, "tm", scatter_dimension=3, tiled=True)
    grad_down = lax.psum(shares, "dp")
    return (encoded, grad_down)


def solution(mesh):
    placed = (P("dp", "tm", None, None, None), P(), P(), P(), P(), P("dp", None, "tm", None, None))
    return jax.shard_map(
        per_device,
        mesh=mesh,
        in_specs=placed,
        out_specs=(P("dp", None, "tm", None, None), P(None, None, None, "tm")),
        check_vma=False,
    )
```

profile of v0, /device:TPU:8, one launch (start us, length us, event | category | flops | bytes accessed | tf_op | source)
XLA Modules:
  0.0 432.3 jit_solution(16287270471883125071)
XLA Ops:
  7.2 2.1 collective-permute-start
  9.3 1.3 fusion.17
  10.6 7.5 %collective-permute-done = bf16[1,2,64,16,128]{4,3,2,1,0:T(8,128)(2,1)S(1)} collective-permute-done((bf16[1,2,64,16,128]{4,3,2,1,0:T(8,128)(2,1)}, bf16[1,2,64,16,128]{4,3,2,1,0:T(8,128)(2,1)S(1)}, u32[]{:S(2)}, u32[]{:S(2)}) %collective-permute-start) | collective-permute-done | bytes 524320 | tf_op jit(solution)/shard_map/ppermute | solution.py:12
  18.2 3.1 pad_slice_fusion.2
  21.3 0.6 pad_slice_fusion.1
  21.9 0.4 pad_maximum_fusion
  22.4 0.6 fusion.18
  22.9 0.6 convolution_add_fusion.7
  23.5 0.4 pad_maximum_fusion.2
  24.0 0.6 convolution_add_fusion.6
  24.6 0.6 convolution_add_fusion.5
  25.1 0.2 pad_maximum_fusion.4
  25.4 0.6 convolution_add_fusion.4
  25.9 0.4 pad_maximum_fusion.5
  26.4 0.6 convolution_add_fusion.3
  27.0 0.6 convolution_add_fusion.2
  27.6 0.4 pad_maximum_fusion.7
  28.0 0.6 convolution_add_fusion.1
  28.6 0.7 fusion.16
  29.3 0.1 reduce_sum.26
  29.4 0.1 reduce_sum.41
  29.5 0.1 reduce_sum.30
  29.6 0.1 reduce_sum.42
  29.7 50.1 %all-reduce.3 = (f32[1,32]{1,0:T(1,128)S(1)}, f32[1,32]{1,0:T(1,128)S(1)}) all-reduce(f32[1,32]{1,0:T(1,128)S(1)} %bitcast.101, f32[1,32]{1,0:T(1,128)S(1)} %bitcast.100), channel_id=1, replica_groups=mesh['dp'=16,'tm'=32] {'tm'}, use_global_device_ids=true, to_apply=%region_5.6 | all-reduce | flops 64 | bytes 512 | tf_op jit(solution)/shard_map/psum | solution.py:58
  80.0 0.1 mul.65
  80.1 0.1 sub.29
  80.3 0.4 multiply_convert_fusion
  80.6 26.8 %all_to_all.18 = bf16[1,2,64,16,128]{4,3,1,0,2:T(8,128)(2,1)S(1)} all-to-all(bf16[1,2,64,16,128]{4,3,1,0,2:T(8,128)(2,1)S(1)} %multiply_convert_fusion), channel_id=1, replica_groups=mesh['dp'=16,'tm'=32] {'tm'}, dimensions={2} | all-to-all | bytes 1048576 | tf_op jit(solution)/shard_map/all_to_all | solution.py:68
  107.5 2.1 collective-permute-start.1
  109.6 3.7 collective-permute-done.1
  113.3 0.2 fusion.2
  113.4 0.4 slice.211
  113.9 0.4 slice.212
  114.3 0.7 slice.213
  115.0 0.4 slice.214
  115.4 0.4 slice.215
  115.8 0.7 slice.216
  116.5 0.4 slice.217
  116.9 0.4 slice.218
  117.4 0.7 slice.219
  118.4 0.6 copy.18
  119.1 0.1 copy-done.2
  119.2 1.3 fusion.14
  120.5 1.3 dynamic-slice
  122.5 1.1 fusion.8
  123.6 218.7 %all-reduce.6.cloned.1.call-done = f32[3,3,128,128]{2,3,1,0:T(8,128)} async-done(((f32[3,3,128,128]{2,3,1,0:T(8,128)}), f32[3,3,128,128]{2,3,1,0:T(8,128)}) %all-reduce.6.cloned.1.call-update) | async-done | bytes 589840
  342.3 0.8 constant_dynamic-slice_fusion
  343.1 82.4 %psum.23 = f32[3,3,128,4]{2,3,1,0:T(4,128)} all-reduce(f32[3,3,128,4]{2,3,1,0:T(4,128)S(1)} %constant_dynamic-slice_fusion), channel_id=1, replica_groups=mesh['dp'=16,'tm'=32] {'dp'}, use_global_device_ids=true, to_apply=%region_7.8 | all-reduce | flops 4608 | bytes 36864 | tf_op jit(solution)/shard_map/psum | solution.py:86
  (27 shorter events, 0.7 us)
Async XLA Ops:
  7.2 115.3 %copy-start = (bf16[3,3,128,128]{3,2,1,0:T(8,128)(2,1)S(1)}, bf16[3,3,128,128]{3,2,1,0:T(8,128)(2,1)}, u32[]{:S(2)}) copy-start(bf16[3,3,128,128]{3,2,1,0:T(8,128)(2,1)} %param.10) | copy-start | bytes 884740
  7.2 10.9 %copy-start.1 = (bf16[1,2,64,16,128]{4,3,2,1,0:T(8,128)(2,1)S(1)}, bf16[1,2,64,16,128]{4,3,2,1,0:T(8,128)(2,1)}, u32[]{:S(2)}) copy-start(bf16[1,2,64,16,128]{4,3,2,1,0:T(8,128)(2,1)} %param.6) | copy-start | bytes 1572868
  7.2 335.1 %all-reduce.6.cloned.1.call-start = ((), (), s32[]{:S(2)}) async-start(), calls=%async_computation.1 | async-start | bytes 1179648
  7.2 10.8 %collective-permute-start = (bf16[1,2,64,16,128]{4,3,2,1,0:T(8,128)(2,1)}, bf16[1,2,64,16,128]{4,3,2,1,0:T(8,128)(2,1)S(1)}, u32[]{:S(2)}, u32[]{:S(2)}) collective-permute-start(bf16[1,2,64,16,128]{4,3,2,1,0:T(8,128)(2,1)} %param.6), channel_id=1, source_target_pairs={{0,1},{1,2},{2,3},{3,4},{4,5},{5,6},{6,7},{7,8},{8,9},{9,10},{10,1... | collective-permute-start | bytes 1572872 | tf_op jit(solution)/shard_map/ppermute | solution.py:12
  28.6 51.7 %copy-start.3 = (f32[128]{0:T(128)S(1)}, f32[128]{0:T(128)}, u32[]{:S(2)}) copy-start(f32[128]{0:T(128)} %param.9) | copy-start | bytes 1540
  28.6 51.7 %copy-start.4 = (f32[128]{0:T(128)S(1)}, f32[128]{0:T(128)}, u32[]{:S(2)}) copy-start(f32[128]{0:T(128)} %param.8) | copy-start | bytes 1540
  107.5 5.8 %collective-permute-start.1 = (bf16[1,64,1,16,128]{4,3,1,2,0:T(8,128)(2,1)S(1)}, bf16[1,64,1,16,128]{4,3,1,2,0:T(8,128)(2,1)S(1)}, u32[]{:S(2)}, u32[]{:S(2)}) collective-permute-start(bf16[1,64,1,16,128]{4,3,1,2,0:T(8,128)(2,1)S(1)} %slice.221), channel_id=1, source_target_pairs={{1,0},{2,1},{3,2},{4,3},{5,4},{6,5},{7,6},{8,7},{9,8},{10,9},{11,1... | collective-permute-start | bytes 786440 | tf_op jit(solution)/shard_map/ppermute | solution.py:12
  118.3 0.9 copy-start.2
Sparse Core Ops, SparseCore 0:
  120.7 221.6 all-reduce.5
where the time goes:
time: 433 us; the launch traced here: 432 us
  waiting for transfers between devices  230 us (53%)
  blocking collectives  159 us (37%)
  between operations  15.1 us (3%)
  local copies, waits for them, and re-layouts  13.4 us (3%)
  matrix products  7.8 us (2%)
    unnamed x2, waiting for transfers between devices  219 us
    psum x1, blocking collectives, per_device(): grad_down = lax.psum(shares, 'dp')  82.4 us
    psum x1, blocking collectives, per_device(): group_sums, group_squares = lax.psum((group_sums, group_squares), 'tm')  50.1 us
    all_to_all x1, blocking collectives, per_device(): lax.all_to_all(hidden, 'tm', split_axis=2, concat_axis=1, tiled=True)  26.8 us
    ppermute x2, waiting for transfers between devices, passed_along(): return lax.ppermute(shard, axis, pairs)  11.1 us
  transfers between devices with their start and end apart: 3, of which 3 were waited for; matrix products, arithmetic and copies ran while one was open for 1% of the time, Pallas kernels for 0%

commit v1 on v0

v1 whole, which is shorter than its diff:
```python
import jax
import jax.numpy as jnp
from jax import lax
from jax.sharding import PartitionSpec as P

G = 32


def passed_along(shard, axis, by):
    count = lax.axis_size(axis)
    pairs = [(i, i + by) for i in range(count) if 0 <= i + by < count]
    return lax.ppermute(shard, axis, pairs)


def from_all(value, axis):
    count = lax.axis_size(axis)
    copies = jnp.broadcast_to(value[None], (count, *value.shape))
    return lax.all_to_all(copies, axis, split_axis=0, concat_axis=0, tiled=True)


def per_device(activations, conv_weight, norm_gain, norm_bias, down_weight, cotangent):
    clip_count, frames_dev, height, width_cells, channels = activations.shape
    out_channels = conv_weight.shape[-1]
    members_tm = lax.axis_size("tm")
    groups = G
    per_group = channels // groups
    earlier = passed_along(activations, "tm", 1)
    cot = lax.all_to_all(cotangent, "tm", split_axis=1, concat_axis=2, tiled=True)
    framed = jnp.concatenate([earlier, activations], axis=1)
    framed = jnp.pad(framed, ((0, 0), (0, 0), (1, 1), (1, 1), (0, 0)))
    conv_out = jnp.zeros(
        (clip_count * frames_dev * height * width_cells, out_channels), jnp.float32
    )
    for row_tap in range(3):
        for col_tap in range(3):
            window_slab = framed[
                :, :, row_tap : row_tap + height, col_tap : col_tap + width_cells, :
            ]
            stacked = jnp.concatenate(
                [window_slab[:, time_tap : time_tap + frames_dev] for time_tap in range(3)], axis=-1
            )
            tap_weight = conv_weight[:, row_tap, col_tap].reshape(3 * channels, out_channels)
            conv_out = conv_out + jnp.dot(
                stacked.reshape(-1, 3 * channels), tap_weight, preferred_element_type=jnp.float32
            )
    sums = jnp.stack([jnp.sum(conv_out, axis=0), jnp.sum(conv_out * conv_out, axis=0)])
    sums = jnp.sum(from_all(sums, "tm"), axis=0)
    group_sums, group_squares = jnp.sum(sums.reshape(2, groups, per_group), axis=-1)
    members = float(frames_dev * members_tm * height * width_cells * per_group)
    group_mean = group_sums / members
    variance = group_squares / members - group_mean * group_mean
    inverse = lax.rsqrt(variance + 1e-06)
    mean_c = jnp.repeat(group_mean, per_group)
    inverse_c = jnp.repeat(inverse, per_group)
    normed = (conv_out - mean_c) * inverse_c * norm_gain + norm_bias
    hidden = jax.nn.silu(normed).astype(jnp.bfloat16)
    hidden = hidden.reshape(frames_dev, height, width_cells, channels)
    extended = jnp.pad(hidden, ((0, 0), (0, 1), (0, 1), (0, 0)))
    rows_out, cols_out = height // 2, width_cells // 2
    patches = jnp.concatenate(
        [
            extended[
                :, p : p + 2 * rows_out - 1 : 2, q : q + 2 * cols_out - 1 : 2, :
            ]
            for p in range(3)
            for q in range(3)
        ],
        axis=-1,
    ).reshape(-1, 9 * channels)
    encoded = (
        jnp.dot(patches, down_weight.reshape(9 * channels, -1), preferred_element_type=jnp.float32)
        .astype(jnp.bfloat16)
        .reshape(clip_count, frames_dev, rows_out, cols_out, out_channels)
    )
    encoded = lax.all_to_all(encoded, "tm", split_axis=2, concat_axis=1, tiled=True)
    partial_value = lax.dot_general(
        cot.reshape(-1, out_channels),
        patches,
        (((0,), (0,)), ((), ())),
        preferred_element_type=jnp.float32,
    )
    own = out_channels // members_tm
    shares = partial_value.reshape(members_tm, own, 9 * channels)
    shares = lax.all_to_all(shares, "tm", split_axis=0, concat_axis=0, tiled=True)
    shares = jnp.sum(shares, axis=0)
    total = jnp.sum(from_all(shares, "dp"), axis=0)
    grad_down = total.T.reshape(3, 3, channels, own)
    return (encoded, grad_down)


def solution(mesh):
    placed = (P("dp", "tm", None, None, None), P(), P(), P(), P(), P("dp", None, "tm", None, None))
    return jax.shard_map(
        per_device,
        mesh=mesh,
        in_specs=placed,
        out_specs=(P("dp", None, "tm", None, None), P(None, None, None, "tm")),
        check_vma=False,
    )
```

time: 433 us -> 126 us (0.29)
  the two profiles are of different devices: /device:TPU:8 before, /device:TPU:1 now
where the time goes in v1:
time: 126 us
  waiting for transfers between devices  46.2 us (37%)
  starting transfers between devices  43 us (34%)
  local copies, waits for them, and re-layouts  25.8 us (20%)
  matrix products  6.23 us (5%)
  other arithmetic  3.16 us (3%)
    all_to_all x2, waiting for transfers between devices, from_all(): return lax.all_to_all(copies, axis, split_axis=0, concat_axis=0, tiled=True)  20.6 us
    all_to_all x2, starting transfers between devices, from_all(): return lax.all_to_all(copies, axis, split_axis=0, concat_axis=0, tiled=True)  20 us
    all_to_all x1, waiting for transfers between devices, per_device(): lax.all_to_all(shares, 'tm', split_axis=0, concat_axis=0, tiled=True)  16.7 us
    slice x9, local copies, waits for them, and re-layouts, per_device(): extended[:, p:p + 2 * rows_out - 1:2, q:q + 2 * cols_out - 1:2, :]  16 us
    all_to_all x1, waiting for transfers between devices, per_device(): lax.all_to_all(encoded, 'tm', split_axis=2, concat_axis=1, tiled=True)  8.98 us
    all_to_all x1, starting transfers between devices, per_device(): lax.all_to_all(cotangent, 'tm', split_axis=1, concat_axis=2, tiled=True)  8.29 us
    all_to_all x1, starting transfers between devices, per_device(): lax.all_to_all(encoded, 'tm', split_axis=2, concat_axis=1, tiled=True)  5.59 us
    dot_general x9, matrix products, per_device(): jnp.dot(stacked.reshape(-1, 3 * channels), tap_weight, preferred_element_...  5.36 us
  transfers between devices with their start and end apart: 6, of which 4 were waited for; matrix products, arithmetic and copies ran while one was open for 11% of the time, Pallas kernels for 0%

profile of v1, /device:TPU:1, one launch (start us, length us, event | category | flops | bytes accessed | tf_op | source)
XLA Modules:
  0.0 125.5 jit_solution(1272603998059128985)
XLA Ops:
  0.7 4.7 %collective-permute-start = (bf16[1,2,64,16,128]{4,3,2,1,0:T(8,128)(2,1)}, bf16[1,2,64,16,128]{4,3,2,1,0:T(8,128)(2,1)S(1)}, u32[]{:S(2)}, u32[]{:S(2)}) collective-permute-start(bf16[1,2,64,16,128]{4,3,2,1,0:T(8,128)(2,1)} %param.6), channel_id=1, source_target_pairs={{0,1},{1,2},{2,3},{3,4},{4,5},{5,6},{6,7},{7,8},{8,9},{9,10},{10,1... | collective-permute-start | bytes 1572872 | tf_op jit(solution)/shard_map/ppermute | solution.py:12
  5.4 8.3 %all-to-all-start.2 = ((bf16[1,64,1,8,128]{4,3,2,0,1:T(8,128)(2,1)}), bf16[1,64,1,8,128]{4,3,2,0,1:T(8,128)(2,1)S(1)}, u32[]{:S(2)}, u32[]{:S(2)}) async-start(bf16[1,64,1,8,128]{4,3,2,0,1:T(8,128)(2,1)} %bitcast.99), calls=%async_computation.2 | async-start | bytes 262144 | tf_op jit(solution)/shard_map/all_to_all | solution.py:28
  13.7 1.3 %fusion.3 = (bf16[3,1,1,128,128]{4,3,2,1,0:T(8,128)(2,1)S(1)}, bf16[3,1,1,128,128]{4,3,2,1,0:T(8,128)(2,1)S(1)}, bf16[3,1,1,128,128]{4,3,2,1,0:T(8,128)(2,1)S(1)...) fusion(bf16[3,3,3,128,128]{4,3,2,1,0:T(8,128)(2,1)} %param.7), kind=kLoop, calls=%fused_computation.62 | loop fusion | bytes 1769472 | tf_op jit(solution)/shard_map/slice | solution.py:42
  15.1 3.1 %pad_slice_fusion.2 = (bf16[1,2,64,16,128]{4,3,2,1,0:T(8,128)(2,1)S(1)}, bf16[1,2,64,16,128]{4,3,2,1,0:T(8,128)(2,1)S(1)}, bf16[1,2,64,16,128]{4,3,2,1,0:T(8,128...) fusion(bf16[1,4,64,16,128]{4,3,2,1,0:T(8,128)(2,1)S(1)} %consta, ...), kind=kLoop, calls=%fused_computation.2 | loop fusion | bytes 11010048 | tf_op jit(solution)/shard_map/slice | solution.py:40
  18.3 0.6 pad_slice_fusion.1
  18.9 0.4 pad_maximum_fusion
  19.3 0.6 fusion.4
  19.9 0.6 convolution_add_fusion.7
  20.5 0.4 pad_maximum_fusion.2
  20.9 0.6 convolution_add_fusion.6
  21.5 0.6 convolution_add_fusion.5
  22.1 0.2 pad_maximum_fusion.4
  22.3 0.6 convolution_add_fusion.4
  22.9 0.4 pad_maximum_fusion.5
  23.3 0.6 convolution_add_fusion.3
  23.9 0.6 convolution_add_fusion.2
  24.5 0.4 pad_maximum_fusion.7
  24.9 0.6 convolution_add_fusion.1
  25.5 0.7 fusion.2
  26.3 0.6 broadcast_in_dim.8
  26.9 8.3 %all-to-all-start = ((f32[32,2,128]{2,1,0:T(2,128)}), f32[32,2,128]{2,1,0:T(2,128)S(1)}, u32[]{:S(2)}, u32[]{:S(2)}) async-start(f32[32,2,128]{2,1,0:T(2,128)} %broadcast_in_dim.8), calls=%async_computation | async-start | bytes 65536 | tf_op jit(solution)/shard_map/all_to_all | solution.py:18
  35.2 7.9 %all-to-all-done = f32[32,2,128]{2,1,0:T(2,128)S(1)} async-done(((f32[32,2,128]{2,1,0:T(2,128)}), f32[32,2,128]{2,1,0:T(2,128)S(1)}, u32[]{:S(2)}, u32[]{:S(2)}) %all-to-all-start) | async-done | bytes 32800 | tf_op jit(solution)/shard_map/all_to_all | solution.py:18
  43.5 0.1 mul.30
  43.6 0.1 sub.13
  43.8 0.4 multiply_convert_fusion
  44.1 0.1 pad.9
  44.3 1.4 %slice.198 = bf16[2,32,8,128]{3,2,1,0:T(8,128)(2,1)S(1)} slice(bf16[2,65,17,128]{3,2,1,0:T(8,128)(2,1)S(1)} %pad.9), slice={[0:2:1], [0:63:2], [0:15:2], [0:128:1]} | slice | bytes 262144 | tf_op jit(solution)/shard_map/slice | solution.py:62
  45.7 1.4 %slice.199 = bf16[2,32,8,128]{3,2,1,0:T(8,128)(2,1)S(1)} slice(bf16[2,65,17,128]{3,2,1,0:T(8,128)(2,1)S(1)} %pad.9), slice={[0:2:1], [0:63:2], [1:16:2], [0:128:1]} | slice | bytes 262144 | tf_op jit(solution)/shard_map/slice | solution.py:62
  47.0 1.5 %slice.200 = bf16[2,32,8,128]{3,2,1,0:T(8,128)(2,1)S(1)} slice(bf16[2,65,17,128]{3,2,1,0:T(8,128)(2,1)S(1)} %pad.9), slice={[0:2:1], [0:63:2], [2:17:2], [0:128:1]} | slice | bytes 262144 | tf_op jit(solution)/shard_map/slice | solution.py:62
  48.5 1.4 %slice.201 = bf16[2,32,8,128]{3,2,1,0:T(8,128)(2,1)S(1)} slice(bf16[2,65,17,128]{3,2,1,0:T(8,128)(2,1)S(1)} %pad.9), slice={[0:2:1], [1:64:2], [0:15:2], [0:128:1]} | slice | bytes 262144 | tf_op jit(solution)/shard_map/slice | solution.py:62
  50.0 1.4 %slice.202 = bf16[2,32,8,128]{3,2,1,0:T(8,128)(2,1)S(1)} slice(bf16[2,65,17,128]{3,2,1,0:T(8,128)(2,1)S(1)} %pad.9), slice={[0:2:1], [1:64:2], [1:16:2], [0:128:1]} | slice | bytes 262144 | tf_op jit(solution)/shard_map/slice | solution.py:62
  51.4 1.5 %slice.203 = bf16[2,32,8,128]{3,2,1,0:T(8,128)(2,1)S(1)} slice(bf16[2,65,17,128]{3,2,1,0:T(8,128)(2,1)S(1)} %pad.9), slice={[0:2:1], [1:64:2], [2:17:2], [0:128:1]} | slice | bytes 262144 | tf_op jit(solution)/shard_map/slice | solution.py:62
  52.9 2.3 %slice.204 = bf16[2,32,8,128]{3,2,1,0:T(8,128)(2,1)S(1)} slice(bf16[2,65,17,128]{3,2,1,0:T(8,128)(2,1)S(1)} %pad.9), slice={[0:2:1], [2:65:2], [0:15:2], [0:128:1]} | slice | bytes 262144 | tf_op jit(solution)/shard_map/slice | solution.py:62
  55.2 2.3 %slice.205 = bf16[2,32,8,128]{3,2,1,0:T(8,128)(2,1)S(1)} slice(bf16[2,65,17,128]{3,2,1,0:T(8,128)(2,1)S(1)} %pad.9), slice={[0:2:1], [2:65:2], [1:16:2], [0:128:1]} | slice | bytes 262144 | tf_op jit(solution)/shard_map/slice | solution.py:62
  57.5 2.9 %slice.206 = bf16[2,32,8,128]{3,2,1,0:T(8,128)(2,1)S(1)} slice(bf16[2,65,17,128]{3,2,1,0:T(8,128)(2,1)S(1)} %pad.9), slice={[0:2:1], [2:65:2], [2:17:2], [0:128:1]} | slice | bytes 262144 | tf_op jit(solution)/shard_map/slice | solution.py:62
  60.7 0.4 convolution_bitcast_fusion
  61.1 1.0 reshape.81
  62.1 4.5 %all-to-all-start.3 = ((f32[32,4,1152]{2,1,0:T(4,128)}), f32[32,4,1152]{2,1,0:T(4,128)S(1)}, u32[]{:S(2)}, u32[]{:S(2)}) async-start(f32[32,4,1152]{2,1,0:T(4,128)} %reshape.81), calls=%async_computation.3 | async-start | bytes 1179648 | tf_op jit(solution)/shard_map/all_to_all | solution.py:84
  66.6 0.5 convolution_convert_fusion
  67.1 0.7 copy.27
  67.8 16.7 %all-to-all-done.3 = f32[32,4,1152]{2,1,0:T(4,128)S(1)} async-done(((f32[32,4,1152]{2,1,0:T(4,128)}), f32[32,4,1152]{2,1,0:T(4,128)S(1)}, u32[]{:S(2)}, u32[]{:S(2)}) %all-to-all-start.3) | async-done | bytes 589856 | tf_op jit(solution)/shard_map/all_to_all | solution.py:84
  84.4 5.6 %all-to-all-start.1 = ((bf16[1,2,32,8,128]{4,3,1,0,2:T(8,128)(2,1)}), bf16[1,2,32,8,128]{4,3,1,0,2:T(8,128)(2,1)S(1)}, u32[]{:S(2)}, u32[]{:S(2)}) async-start(bf16[1,2,32,8,128]{4,3,1,0,2:T(8,128)(2,1)} %copy.27), calls=%async_computation.1 | async-start | bytes 262144 | tf_op jit(solution)/shard_map/all_to_all | solution.py:75
  90.1 9.0 %all-to-all-done.1 = bf16[1,2,32,8,128]{4,3,1,0,2:T(8,128)(2,1)S(1)} async-done(((bf16[1,2,32,8,128]{4,3,1,0,2:T(8,128)(2,1)}), bf16[1,2,32,8,128]{4,3,1,0,2:T(8,128)(2,1)S(1)}, u32[]{:S(2)}, u32[]{:S(2)}) %all-to-all-start.1) | async-done | bytes 131104 | tf_op jit(solution)/shard_map/all_to_all | solution.py:75
  99.1 0.7 broadcast_in_dim.11
  99.9 11.7 %all-to-all-start.4 = ((f32[16,4,1152]{2,1,0:T(4,128)}), f32[16,4,1152]{2,1,0:T(4,128)S(1)}, u32[]{:S(2)}, u32[]{:S(2)}) async-start(f32[16,4,1152]{2,1,0:T(4,128)} %broadcast_in_dim.11), calls=%async_computation.4 | async-start | bytes 589824 | tf_op jit(solution)/shard_map/all_to_all | solution.py:18
  111.6 12.7 %all-to-all-done.4 = f32[16,4,1152]{2,1,0:T(4,128)S(1)} async-done(((f32[16,4,1152]{2,1,0:T(4,128)}), f32[16,4,1152]{2,1,0:T(4,128)S(1)}, u32[]{:S(2)}, u32[]{:S(2)}) %all-to-all-start.4) | async-done | bytes 294944 | tf_op jit(solution)/shard_map/all_to_all | solution.py:18
  124.2 0.7 reduce_sum.59
  124.9 0.7 copy.44
  (31 shorter events, 0.9 us)
Async XLA Ops:
  0.6 66.0 %copy-start = (bf16[3,3,128,128]{3,2,1,0:T(8,128)(2,1)S(1)}, bf16[3,3,128,128]{3,2,1,0:T(8,128)(2,1)}, u32[]{:S(2)}) copy-start(bf16[3,3,128,128]{3,2,1,0:T(8,128)(2,1)} %param.10) | copy-start | bytes 884740
  0.6 14.4 %copy-start.1 = (bf16[1,2,64,16,128]{4,3,2,1,0:T(8,128)(2,1)S(1)}, bf16[1,2,64,16,128]{4,3,2,1,0:T(8,128)(2,1)}, u32[]{:S(2)}) copy-start(bf16[1,2,64,16,128]{4,3,2,1,0:T(8,128)(2,1)} %param.6) | copy-start | bytes 1572868
  0.7 14.3 %collective-permute-start = (bf16[1,2,64,16,128]{4,3,2,1,0:T(8,128)(2,1)}, bf16[1,2,64,16,128]{4,3,2,1,0:T(8,128)(2,1)S(1)}, u32[]{:S(2)}, u32[]{:S(2)}) collective-permute-start(bf16[1,2,64,16,128]{4,3,2,1,0:T(8,128)(2,1)} %param.6), channel_id=1, source_target_pairs={{0,1},{1,2},{2,3},{3,4},{4,5},{5,6},{6,7},{7,8},{8,9},{9,10},{10,1... | collective-permute-start | bytes 1572872 | tf_op jit(solution)/shard_map/ppermute | solution.py:12
  5.4 20.9 %all-to-all-start.2 = ((bf16[1,64,1,8,128]{4,3,2,0,1:T(8,128)(2,1)}), bf16[1,64,1,8,128]{4,3,2,0,1:T(8,128)(2,1)S(1)}, u32[]{:S(2)}, u32[]{:S(2)}) async-start(bf16[1,64,1,8,128]{4,3,2,0,1:T(8,128)(2,1)} %bitcast.99), calls=%async_computation.2 | async-start | bytes 262144 | tf_op jit(solution)/shard_map/all_to_all | solution.py:28
  25.5 18.2 %copy-start.2 = (f32[128]{0:T(128)S(1)}, f32[128]{0:T(128)}, u32[]{:S(2)}) copy-start(f32[128]{0:T(128)} %param.9) | copy-start | bytes 1540
  25.5 18.2 %copy-start.3 = (f32[128]{0:T(128)S(1)}, f32[128]{0:T(128)}, u32[]{:S(2)}) copy-start(f32[128]{0:T(128)} %param.8) | copy-start | bytes 1540
  26.9 16.2 %all-to-all-start = ((f32[32,2,128]{2,1,0:T(2,128)}), f32[32,2,128]{2,1,0:T(2,128)S(1)}, u32[]{:S(2)}, u32[]{:S(2)}) async-start(f32[32,2,128]{2,1,0:T(2,128)} %broadcast_in_dim.8), calls=%async_computation | async-start | bytes 65536 | tf_op jit(solution)/shard_map/all_to_all | solution.py:18
  62.1 22.3 %all-to-all-start.3 = ((f32[32,4,1152]{2,1,0:T(4,128)}), f32[32,4,1152]{2,1,0:T(4,128)S(1)}, u32[]{:S(2)}, u32[]{:S(2)}) async-start(f32[32,4,1152]{2,1,0:T(4,128)} %reshape.81), calls=%async_computation.3 | async-start | bytes 1179648 | tf_op jit(solution)/shard_map/all_to_all | solution.py:84
  84.4 14.7 %all-to-all-start.1 = ((bf16[1,2,32,8,128]{4,3,1,0,2:T(8,128)(2,1)}), bf16[1,2,32,8,128]{4,3,1,0,2:T(8,128)(2,1)S(1)}, u32[]{:S(2)}, u32[]{:S(2)}) async-start(bf16[1,2,32,8,128]{4,3,1,0,2:T(8,128)(2,1)} %copy.27), calls=%async_computation.1 | async-start | bytes 262144 | tf_op jit(solution)/shard_map/all_to_all | solution.py:75
  99.9 24.3 %all-to-all-start.4 = ((f32[16,4,1152]{2,1,0:T(4,128)}), f32[16,4,1152]{2,1,0:T(4,128)S(1)}, u32[]{:S(2)}, u32[]{:S(2)}) async-start(f32[16,4,1152]{2,1,0:T(4,128)} %broadcast_in_dim.11), calls=%async_computation.4 | async-start | bytes 589824 | tf_op jit(solution)/shard_map/all_to_all | solution.py:18

commit v2 on v0

v2 whole, which is shorter than its diff:
```python
import functools

import jax
import jax.numpy as jnp
from jax import lax
from jax.experimental import pallas as pl
from jax.experimental.pallas import tpu as pltpu
from jax.sharding import PartitionSpec as P

GROUP_SIZE = 4
MESH = pl.DeviceIdType.MESH
Z_PART = 4
VMEM = pl.BlockSpec(memory_space=pltpu.VMEM)


def passed_along(shard, axis, by):
    count = lax.axis_size(axis)
    pairs = [(i, i + by) for i in range(count) if 0 <= i + by < count]
    return lax.ppermute(shard, axis, pairs)


def conv_kernel(height, width, earlier_ref, now_ref, weight_ref, out_ref, lanes_ref, wide_ref):
    cells = height * width
    c = 128
    edge = jnp.zeros((width, 4 * c), jnp.bfloat16)
    lanes_ref[pl.ds(0, width), :] = edge
    lanes_ref[pl.ds(cells + width, width), :] = edge
    for frame in range(4):
        source = earlier_ref if frame < 2 else now_ref
        lanes_ref[pl.ds(width, cells), frame * c : (frame + 1) * c] = source[frame % 2]
    zero = jnp.zeros((c, c), jnp.bfloat16)
    for p in range(3):
        for frame in range(4):
            for t in range(2):
                for q in range(3):
                    a = frame - t
                    block = weight_ref[a, p, q] if 0 <= a <= 2 else zero
                    column = (t * 3 + q) * c
                    wide_ref[p, frame * c : (frame + 1) * c, column : column + c] = block
    rows = 16 * width
    column = lax.broadcasted_iota(jnp.int32, (rows, c), 0) % width

    def chunk(step, carry):
        start = pl.multiple_of(step * rows, rows)
        z = jnp.zeros((rows, 6 * c), jnp.float32)
        for p in range(3):
            z = z + jnp.dot(
                lanes_ref[pl.ds(pl.multiple_of(start + p * width, width), rows), :],
                wide_ref[p],
                preferred_element_type=jnp.float32,
            )
        for t in range(2):
            left, middle, right = (z[:, (t * 3 + q) * c : (t * 3 + q + 1) * c] for q in range(3))
            left = jnp.where(column == 0, 0.0, pltpu.roll(left, 1, 0))
            right = jnp.where(column == width - 1, 0.0, pltpu.roll(right, rows - 1, 0))
            out_ref[pl.ds(pl.multiple_of(t * cells + start, rows), rows), :] = left + middle + right
        return carry

    lax.fori_loop(0, height // 16, chunk, 0)


def mid_kernel(
    n_tm, n_dp, height, width, piece,
    conv_ref, gain_ref, bias_ref, down_ref, cot_ref,
    enc_out, grad_out,
    stat_src, stat_buf, patches, enc_src, enc_buf, grad_all, grad_wide, grad_src, grad_buf,
    x_src, x_buf, z_src, z_buf,
    stat_send, stat_recv, enc_send, enc_recv, grad_send, grad_recv, x_send, x_recv, z_send, z_recv,
):
    c = 128
    own = c // n_tm
    n_x = n_dp // Z_PART
    me = lax.axis_index("tm")
    dp = lax.axis_index("dp")
    my_x, my_z = dp // Z_PART, dp % Z_PART

    def tm_peer(d):
        return {"tm": lax.rem(me + d, n_tm)}

    def x_peer(d):
        return {"dp": lax.rem(my_x + d, n_x) * Z_PART + my_z}

    def z_peer(d):
        return {"dp": my_x * Z_PART + lax.rem(my_z + d, Z_PART)}

    barrier = pltpu.get_barrier_semaphore()

    def greet(d, carry):
        pl.semaphore_signal(barrier, inc=1, device_id=tm_peer(d), device_id_type=MESH)
        return carry

    lax.fori_loop(1, n_tm, greet, 0)
    for d in range(1, n_x):
        pl.semaphore_signal(barrier, inc=1, device_id=x_peer(d), device_id_type=MESH)
    for d in range(1, Z_PART):
        pl.semaphore_signal(barrier, inc=1, device_id=z_peer(d), device_id_type=MESH)

    conv = conv_ref[...]
    local = jnp.concatenate(
        [
            jnp.sum(conv, axis=0, keepdims=True),
            jnp.sum(conv * conv, axis=0, keepdims=True),
            jnp.zeros((6, c), jnp.float32),
        ],
        axis=0,
    )
    stat_src[...] = local
    stat_buf[me] = local
    pl.semaphore_wait(barrier, n_tm - 1 + n_x - 1 + Z_PART - 1)

    def exchange(size, peer, mine, src_of, dst_of, send, recv):
        def sender(d):
            target = lax.rem(mine + d, size)
            return pltpu.make_async_remote_copy(
                src_ref=src_of(target), dst_ref=dst_of(mine), send_sem=send.at[d],
                recv_sem=recv.at[mine], device_id=peer(d), device_id_type=MESH,
            )

        def receiver(d):
            origin = lax.rem(mine + size - d, size)
            return pltpu.make_async_remote_copy(
                src_ref=src_of(origin), dst_ref=dst_of(origin), send_sem=send.at[d],
                recv_sem=recv.at[origin], device_id=peer(d), device_id_type=MESH,
            )

        def loop(act):
            def step(d, carry):
                act(d)
                return carry

            lax.fori_loop(1, size, step, 0)

        loop(lambda d: sender(d).start())
        return (
            lambda: loop(lambda d: receiver(d).wait_recv()),
            lambda: loop(lambda d: sender(d).wait_send()),
        )

    stats_here, stats_gone = exchange(
        n_tm, tm_peer, me, lambda i: stat_src, lambda i: stat_buf.at[i], stat_send, stat_recv
    )
    stats_here()
    sums = jnp.sum(stat_buf[...], axis=0)
    lane = lax.broadcasted_iota(jnp.int32, (8, c), 1)
    for reach in (1, 2):
        partner = jnp.where(
            lane % (2 * reach) < reach, pltpu.roll(sums, c - reach, 1), pltpu.roll(sums, reach, 1)
        )
        sums = sums + partner
    members = float(n_tm * 2 * height * width * GROUP_SIZE)
    mean = sums[0:1] / members
    variance = sums[1:2] / members - mean * mean
    scale = lax.rsqrt(variance + 1e-06)
    gain, bias = gain_ref[...], bias_ref[...]

    half_w, half_h = width // 2, height // 2
    rows_half = height * half_w

    def hidden_at(parity):
        frames = []
        for t in range(2):
            x = conv_ref[pl.ds(t * height * width + parity, rows_half, stride=2), :]
            y = (x - mean) * scale * gain + bias
            y = y / (1.0 + jnp.exp(-y))
            y = y.astype(jnp.bfloat16).astype(jnp.float32)
            frames.append(y.reshape(half_h, 2, 1, half_w, c))
        return jnp.concatenate(frames, axis=2)

    even, odd = hidden_at(0), hidden_at(1)
    flat = even.reshape(-1, half_w, c)
    place = lax.broadcasted_iota(jnp.int32, flat.shape, 1)
    shifted = jnp.where(place == half_w - 1, 0.0, pltpu.roll(flat, half_w - 1, 1)).reshape(even.shape)
    for q, source in enumerate((even, odd, shifted)):
        upper, lower = source[:, 0], source[:, 1]
        below = jnp.concatenate([upper[1:], jnp.zeros_like(upper[:1])], axis=0)
        for p, rows in enumerate((upper, lower, below)):
            at = (p * 3 + q) * c
            patches[:, at : at + c] = rows.reshape(-1, c).astype(jnp.bfloat16)

    partial_grad = lax.dot_general(
        cot_ref[...], patches[...], (((0,), (0,)), ((), ())), preferred_element_type=jnp.float32
    )
    for tap in range(9):
        grad_all[tap] = partial_grad[:, tap * c : (tap + 1) * c]
    grad_wide[...] = jnp.zeros_like(grad_wide)
    for tap in range(9):
        for j in range(own):
            grad_wide[pl.ds(tap * own + j, n_tm, stride=piece), :] = grad_all[
                tap, pl.ds(j, n_tm, stride=own), :
            ]
    grad_src[...] = grad_wide[...].astype(jnp.bfloat16)
    grad_here, grad_gone = exchange(
        n_tm, tm_peer, me,
        lambda i: grad_src.at[pl.ds(pl.multiple_of(i * piece, piece), piece)],
        lambda i: grad_buf.at[pl.ds(pl.multiple_of(i * piece, piece), piece)],
        grad_send, grad_recv,
    )
    here = pl.ds(pl.multiple_of(me * piece, piece), piece)
    grad_buf[here, :] = grad_src[here, :]

    enc = 2 * half_w
    enc_src[...] = jnp.dot(
        patches[...], down_ref[...], preferred_element_type=jnp.float32
    ).astype(jnp.bfloat16)
    enc_here, enc_gone = exchange(
        n_tm, tm_peer, me,
        lambda i: enc_src.at[pl.ds(pl.multiple_of(i * enc, enc), enc)],
        lambda i: enc_buf.at[pl.ds(pl.multiple_of(i * enc, enc), enc)],
        enc_send, enc_recv,
    )
    mine = pl.ds(pl.multiple_of(me * enc, enc), enc)
    enc_buf[mine, :] = enc_src[mine, :]

    grad_here()
    total = jnp.zeros((piece, c), jnp.float32)
    for i in range(n_tm):
        total = total + grad_buf[pl.ds(i * piece, piece), :].astype(jnp.float32)
    x_src[...] = total
    x_buf[my_x] = total
    x_here, x_gone = exchange(
        n_x, x_peer, my_x, lambda i: x_src, lambda i: x_buf.at[i], x_send, x_recv
    )
    x_here()
    total = jnp.sum(x_buf[...], axis=0)
    z_src[...] = total
    z_buf[my_z] = total
    z_here, z_gone = exchange(
        Z_PART, z_peer, my_z, lambda i: z_src, lambda i: z_buf.at[i], z_send, z_recv
    )
    enc_here()
    enc_out[...] = enc_buf[...]
    z_here()
    grad_out[...] = jnp.sum(z_buf[...], axis=0)
    for gone in (stats_gone, grad_gone, enc_gone, x_gone, z_gone):
        gone()


def per_device(activations, conv_weight, norm_gain, norm_bias, down_weight, cotangent):
    _, frames_dev, height, width, c = activations.shape
    n_tm, n_dp = lax.axis_size("tm"), lax.axis_size("dp")
    cells = height * width
    positions = frames_dev * cells // 4
    own = c // n_tm
    piece = -(-9 * own // 16) * 16
    earlier = passed_along(activations, "tm", 1)
    cot = lax.all_to_all(
        cotangent.reshape(positions, c), "tm", split_axis=0, concat_axis=0, tiled=True
    )
    conv_out = pl.pallas_call(
        functools.partial(conv_kernel, height, width),
        out_shape=jax.ShapeDtypeStruct((frames_dev * cells, c), jnp.float32),
        in_specs=[VMEM] * 3,
        out_specs=VMEM,
        scratch_shapes=[
            pltpu.VMEM((cells + 2 * width, 4 * c), jnp.bfloat16),
            pltpu.VMEM((3, 4 * c, 6 * c), jnp.bfloat16),
        ],
        name="causal_conv",
    )(
        earlier.reshape(frames_dev, cells, c), activations.reshape(frames_dev, cells, c), conv_weight
    )
    f32, bf16 = jnp.float32, jnp.bfloat16
    n_x = n_dp // Z_PART
    dma = pltpu.SemaphoreType.DMA
    encoded, grad = pl.pallas_call(
        functools.partial(mid_kernel, n_tm, n_dp, height, width, piece),
        out_shape=(
            jax.ShapeDtypeStruct((positions, c), bf16),
            jax.ShapeDtypeStruct((piece, c), f32),
        ),
        in_specs=[VMEM] * 5,
        out_specs=(VMEM, VMEM),
        scratch_shapes=[
            pltpu.VMEM((8, c), f32),
            pltpu.VMEM((n_tm, 8, c), f32),
            pltpu.VMEM((positions, 9 * c), bf16),
            pltpu.VMEM((positions, c), bf16),
            pltpu.VMEM((positions, c), bf16),
            pltpu.VMEM((9, c, c), f32),
            pltpu.VMEM((n_tm * piece, c), f32),
            pltpu.VMEM((n_tm * piece, c), bf16),
            pltpu.VMEM((n_tm * piece, c), bf16),
            pltpu.VMEM((piece, c), f32),
            pltpu.VMEM((n_x, piece, c), f32),
            pltpu.VMEM((piece, c), f32),
            pltpu.VMEM((Z_PART, piece, c), f32),
        ]
        + [dma((n_tm,))] * 6
        + [dma((n_x,))] * 2
        + [dma((Z_PART,))] * 2,
        compiler_params=pltpu.CompilerParams(collective_id=0, has_side_effects=True),
        name="norm_down_grad",
    )(
        conv_out,
        norm_gain.reshape(1, c),
        norm_bias.reshape(1, c),
        down_weight.reshape(9 * c, c),
        cot,
    )
    grad_down = grad[: 9 * own].reshape(9, own, c).transpose(0, 2, 1).reshape(3, 3, c, own)
    return encoded.reshape(cotangent.shape), grad_down


def solution(mesh):
    placed = (P("dp", "tm", None, None, None), P(), P(), P(), P(), P("dp", None, "tm", None, None))
    return jax.shard_map(
        per_device,
        mesh=mesh,
        in_specs=placed,
        out_specs=(P("dp", None, "tm", None, None), P(None, None, None, "tm")),
        check_vma=False,
    )
```

time: 433 us -> 71.9 us (0.17)
  the two profiles are of different devices: /device:TPU:8 before, /device:TPU:1 now
where the time goes in v2:
time: 71.9 us; the launch traced here: 71.5 us
  Pallas kernels  51.5 us (72%)
  starting transfers between devices  12.9 us (18%)
  local copies, waits for them, and re-layouts  4.37 us (6%)
  waiting for transfers between devices  2.09 us (3%)
    pallas_call x1, Pallas kernels, per_device(): pl.pallas_call(functools.partial(mid_kernel, n_tm, n_dp, height, width, p...  45.4 us
    all_to_all x1, starting transfers between devices, per_device(): lax.all_to_all(cotangent.reshape(positions, c), 'tm', split_axis=0, conca...  8.29 us
    pallas_call x1, Pallas kernels, per_device(): pl.pallas_call(functools.partial(conv_kernel, height, width), out_shape=j...  6.09 us
    ppermute x1, starting transfers between devices, passed_along(): return lax.ppermute(shard, axis, pairs)  4.58 us
    unnamed x5, local copies, waits for them, and re-layouts  3.02 us
    all_to_all x1, waiting for transfers between devices, per_device(): lax.all_to_all(cotangent.reshape(positions, c), 'tm', split_axis=0, conca...  2.09 us
  transfers between devices with their start and end apart: 2, of which 1 were waited for; matrix products, arithmetic and copies ran while one was open for 0% of the time, Pallas kernels for 9%

profile of v2, /device:TPU:1, one launch (start us, length us, event | category | flops | bytes accessed | tf_op | source)
XLA Modules:
  0.0 71.5 jit_solution(905995900125869451)
XLA Ops:
  0.6 4.6 %collective-permute-start = (bf16[1,2,64,16,128]{4,3,2,1,0:T(8,128)(2,1)}, bf16[1,2,64,16,128]{4,3,2,1,0:T(8,128)(2,1)S(1)}, u32[]{:S(2)}, u32[]{:S(2)}) collective-permute-start(bf16[1,2,64,16,128]{4,3,2,1,0:T(8,128)(2,1)} %param.6), channel_id=1, source_target_pairs={{0,1},{1,2},{2,3},{3,4},{4,5},{5,6},{6,7},{7,8},{8,9},{9,10},{10,1... | collective-permute-start | bytes 1572872 | tf_op jit(solution)/shard_map/ppermute | solution.py:19
  5.2 8.3 %all-to-all-start = ((bf16[32,16,128]{2,1,0:T(8,128)(2,1)}), bf16[32,16,128]{2,1,0:T(8,128)(2,1)S(1)}, u32[]{:S(2)}, u32[]{:S(2)}) async-start(bf16[32,16,128]{2,1,0:T(8,128)(2,1)} %bitcast.17), calls=%async_computation | async-start | bytes 262144 | tf_op jit(solution)/shard_map/all_to_all | solution.py:246
  13.5 0.0 collective-permute-done
  13.5 0.0 copy-start.1
  13.5 0.8 %copy-done.1 = bf16[1,2,64,16,128]{4,3,2,1,0:T(8,128)(2,1)} copy-done((bf16[1,2,64,16,128]{4,3,2,1,0:T(8,128)(2,1)}, bf16[1,2,64,16,128]{4,3,2,1,0:T(8,128)(2,1)S(1)}, u32[]{:S(2)}) %copy-start.1) | copy-done | bytes 524312
  14.3 6.1 %causal_conv.1.conv_ref = f32[2048,128]{1,0:T(8,128)} custom-call(bf16[2,1024,128]{2,1,0:T(8,128)(2,1)} %bitcast.15, bf16[2,1024,128]{2,1,0:T(8,128)(2,1)} %bitcast.14, bf16[3,3,3,128,128]{4,3,2,1,0:T(8,128)(2,1)} %weight_ref.1), custom_call_target="tpu_custom_call" | custom-call | tf_op jit(solution)/shard_map/causal_conv/pallas_call | solution.py:249
  20.4 2.1 %all-to-all-done = bf16[32,16,128]{2,1,0:T(8,128)(2,1)S(1)} async-done(((bf16[32,16,128]{2,1,0:T(8,128)(2,1)}), bf16[32,16,128]{2,1,0:T(8,128)(2,1)S(1)}, u32[]{:S(2)}, u32[]{:S(2)}) %all-to-all-start) | async-done | bytes 131104 | tf_op jit(solution)/shard_map/all_to_all | solution.py:246
  22.5 0.0 copy-start
  22.5 0.7 copy-done
  23.2 45.4 %norm_down_grad.1 = (bf16[512,128]{1,0:T(8,128)(2,1)}, f32[48,128]{1,0:T(8,128)}) custom-call(f32[2048,128]{1,0:T(8,128)} %causal_conv.1.conv_ref, f32[1,128]{1,0:T(1,128)} %bitcast.20, f32[1,128]{1,0:T(1,128)} %bitcast.21, bf16[1152,128]{1,0:T(8,128)(2,1)} %bitcast.16, bf16[512,128]{1,0:T(8,128)(2,1)} %bitcast.13), custom_call_target="tpu_custom_call" | custom-call | tf_op jit(solution)/shard_map/norm_down_grad/pallas_call | solution.py:265
  68.6 0.7 %slice.3 = f32[36,128]{1,0:T(8,128)S(1)} slice(f32[48,128]{1,0:T(8,128)} %get-tuple-element.5), slice={[0:36], [0:128]} | slice | bytes 36864 | tf_op jit(solution)/shard_map/slice | solution.py:300
  69.4 0.6 reshape.38
  70.0 1.6 %copy.10 = bf16[1,64,1,8,128]{4,3,2,1,0:T(8,128)(2,1)} copy(bf16[1,64,1,8,128]{4,3,2,1,0:T(8,128)(2,1)} %bitcast.18) | data formatting | bytes 262144
Async XLA Ops:
  0.6 12.9 %collective-permute-start = (bf16[1,2,64,16,128]{4,3,2,1,0:T(8,128)(2,1)}, bf16[1,2,64,16,128]{4,3,2,1,0:T(8,128)(2,1)S(1)}, u32[]{:S(2)}, u32[]{:S(2)}) collective-permute-start(bf16[1,2,64,16,128]{4,3,2,1,0:T(8,128)(2,1)} %param.6), channel_id=1, source_target_pairs={{0,1},{1,2},{2,3},{3,4},{4,5},{5,6},{6,7},{7,8},{8,9},{9,10},{10,1... | collective-permute-start | bytes 1572872 | tf_op jit(solution)/shard_map/ppermute | solution.py:19
  5.2 17.3 %all-to-all-start = ((bf16[32,16,128]{2,1,0:T(8,128)(2,1)}), bf16[32,16,128]{2,1,0:T(8,128)(2,1)S(1)}, u32[]{:S(2)}, u32[]{:S(2)}) async-start(bf16[32,16,128]{2,1,0:T(8,128)(2,1)} %bitcast.17), calls=%async_computation | async-start | bytes 262144 | tf_op jit(solution)/shard_map/all_to_all | solution.py:246
  13.5 0.8 %copy-start.1 = (bf16[1,2,64,16,128]{4,3,2,1,0:T(8,128)(2,1)}, bf16[1,2,64,16,128]{4,3,2,1,0:T(8,128)(2,1)S(1)}, u32[]{:S(2)}) copy-start(bf16[1,2,64,16,128]{4,3,2,1,0:T(8,128)(2,1)S(1)} %collective-permute-done) | copy-start | bytes 1572868
  22.5 0.7 copy-start

commit v3 on v2

--- a/solution.py
+++ b/solution.py
@@ -19,7 +19,7 @@
     return lax.ppermute(shard, axis, pairs)
 
 
-def conv_kernel(height, width, earlier_ref, now_ref, weight_ref, out_ref, lanes_ref, wide_ref):
+def convolve(height, width, earlier_ref, now_ref, weight_ref, out_ref, lanes_ref, wide_ref):
     cells = height * width
     c = 128
     edge = jnp.zeros((width, 4 * c), jnp.bfloat16)
@@ -41,6 +41,7 @@
     column = lax.broadcasted_iota(jnp.int32, (rows, c), 0) % width
 
     def chunk(step, carry):
+        sums, squares = carry
         start = pl.multiple_of(step * rows, rows)
         z = jnp.zeros((rows, 6 * c), jnp.float32)
         for p in range(3):
@@ -53,19 +54,24 @@
             left, middle, right = (z[:, (t * 3 + q) * c : (t * 3 + q + 1) * c] for q in range(3))
             left = jnp.where(column == 0, 0.0, pltpu.roll(left, 1, 0))
             right = jnp.where(column == width - 1, 0.0, pltpu.roll(right, rows - 1, 0))
-            out_ref[pl.ds(pl.multiple_of(t * cells + start, rows), rows), :] = left + middle + right
-        return carry
-
-    lax.fori_loop(0, height // 16, chunk, 0)
-
-
-def mid_kernel(
+            value = left + middle + right
+            out_ref[pl.ds(pl.multiple_of(t * cells + start, rows), rows), :] = value
+            value = value.reshape(rows // 8, 8, c)
+            sums = sums + jnp.sum(value, axis=0)
+            squares = squares + jnp.sum(value * value, axis=0)
+        return sums, squares
+
+    none = jnp.zeros((8, c), jnp.float32)
+    return lax.fori_loop(0, height // 16, chunk, (none, none))
+
+
+def block_kernel(
     n_tm, n_dp, height, width, piece,
-    conv_ref, gain_ref, bias_ref, down_ref, cot_ref,
+    earlier_ref, now_ref, weight_ref, gain_ref, bias_ref, down_ref, cot_src,
     enc_out, grad_out,
-    stat_src, stat_buf, patches, enc_src, enc_buf, grad_all, grad_wide, grad_src, grad_buf,
+    lanes_ref, wide_ref, conv_ref, cot_ref, stat_src, stat_buf, patches, enc_src, enc_buf, grad_all, grad_wide, grad_src, grad_buf,
     x_src, x_buf, z_src, z_buf,
-    stat_send, stat_recv, enc_send, enc_recv, grad_send, grad_recv, x_send, x_recv, z_send, z_recv,
+    stat_send, stat_recv, cot_send, cot_recv, enc_send, enc_recv, grad_send, grad_recv, x_send, x_recv, z_send, z_recv,
 ):
     c = 128
     own = c // n_tm
@@ -95,11 +101,13 @@
     for d in range(1, Z_PART):
         pl.semaphore_signal(barrier, inc=1, device_id=z_peer(d), device_id_type=MESH)
 
-    conv = conv_ref[...]
+    own_sums, own_squares = convolve(
+        height, width, earlier_ref, now_ref, weight_ref, conv_ref, lanes_ref, wide_ref
+    )
     local = jnp.concatenate(
         [
-            jnp.sum(conv, axis=0, keepdims=True),
-            jnp.sum(conv * conv, axis=0, keepdims=True),
+            jnp.sum(own_sums, axis=0, keepdims=True),
+            jnp.sum(own_squares, axis=0, keepdims=True),
             jnp.zeros((6, c), jnp.float32),
         ],
         axis=0,
@@ -139,6 +147,16 @@
     stats_here, stats_gone = exchange(
         n_tm, tm_peer, me, lambda i: stat_src, lambda i: stat_buf.at[i], stat_send, stat_recv
     )
+    enc = width
+
+    def block_of(ref):
+        return lambda i: ref.at[pl.ds(pl.multiple_of(i * enc, enc), enc)]
+
+    cot_here, cot_gone = exchange(
+        n_tm, tm_peer, me, block_of(cot_src), block_of(cot_ref), cot_send, cot_recv
+    )
+    mine = pl.ds(pl.multiple_of(me * enc, enc), enc)
+    cot_ref[mine, :] = cot_src[mine, :]
     stats_here()
     sums = jnp.sum(stat_buf[...], axis=0)
     lane = lax.broadcasted_iota(jnp.int32, (8, c), 1)
@@ -177,6 +195,7 @@
             at = (p * 3 + q) * c
             patches[:, at : at + c] = rows.reshape(-1, c).astype(jnp.bfloat16)
 
+    cot_here()
     partial_grad = lax.dot_general(
         cot_ref[...], patches[...], (((0,), (0,)), ((), ())), preferred_element_type=jnp.float32
     )
@@ -198,17 +217,12 @@
     here = pl.ds(pl.multiple_of(me * piece, piece), piece)
     grad_buf[here, :] = grad_src[here, :]
 
-    enc = 2 * half_w
     enc_src[...] = jnp.dot(
         patches[...], down_ref[...], preferred_element_type=jnp.float32
     ).astype(jnp.bfloat16)
     enc_here, enc_gone = exchange(
-        n_tm, tm_peer, me,
-        lambda i: enc_src.at[pl.ds(pl.multiple_of(i * enc, enc), enc)],
-        lambda i: enc_buf.at[pl.ds(pl.multiple_of(i * enc, enc), enc)],
-        enc_send, enc_recv,
-    )
-    mine = pl.ds(pl.multiple_of(me * enc, enc), enc)
+        n_tm, tm_peer, me, block_of(enc_src), block_of(enc_buf), enc_send, enc_recv
+    )
     enc_buf[mine, :] = enc_src[mine, :]
 
     grad_here()
@@ -230,8 +244,10 @@
     enc_here()
     enc_out[...] = enc_buf[...]
     z_here()
-    grad_out[...] = jnp.sum(z_buf[...], axis=0)
-    for gone in (stats_gone, grad_gone, enc_gone, x_gone, z_gone):
+    total = jnp.sum(z_buf[...], axis=0)
+    for tap in range(9):
+        grad_out[tap] = total[tap * own : (tap + 1) * own]
+    for gone in (stats_gone, cot_gone, grad_gone, enc_gone, x_gone, z_gone):
         gone()
 
 
@@ -243,34 +259,22 @@
     own = c // n_tm
     piece = -(-9 * own // 16) * 16
     earlier = passed_along(activations, "tm", 1)
-    cot = lax.all_to_all(
-        cotangent.reshape(positions, c), "tm", split_axis=0, concat_axis=0, tiled=True
-    )
-    conv_out = pl.pallas_call(
-        functools.partial(conv_kernel, height, width),
-        out_shape=jax.ShapeDtypeStruct((frames_dev * cells, c), jnp.float32),
-        in_specs=[VMEM] * 3,
-        out_specs=VMEM,
-        scratch_shapes=[
-            pltpu.VMEM((cells + 2 * width, 4 * c), jnp.bfloat16),
-            pltpu.VMEM((3, 4 * c, 6 * c), jnp.bfloat16),
-        ],
-        name="causal_conv",
-    )(
-        earlier.reshape(frames_dev, cells, c), activations.reshape(frames_dev, cells, c), conv_weight
-    )
     f32, bf16 = jnp.float32, jnp.bfloat16
     n_x = n_dp // Z_PART
     dma = pltpu.SemaphoreType.DMA
     encoded, grad = pl.pallas_call(
-        functools.partial(mid_kernel, n_tm, n_dp, height, width, piece),
+        functools.partial(block_kernel, n_tm, n_dp, height, width, piece),
         out_shape=(
             jax.ShapeDtypeStruct((positions, c), bf16),
-            jax.ShapeDtypeStruct((piece, c), f32),
+            jax.ShapeDtypeStruct((9, own, c), f32),
         ),
-        in_specs=[VMEM] * 5,
+        in_specs=[VMEM] * 7,
         out_specs=(VMEM, VMEM),
         scratch_shapes=[
+            pltpu.VMEM((cells + 2 * width, 4 * c), bf16),
+            pltpu.VMEM((3, 4 * c, 6 * c), bf16),
+            pltpu.VMEM((frames_dev * cells, c), f32),
+            pltpu.VMEM((positions, c), bf16),
             pltpu.VMEM((8, c), f32),
             pltpu.VMEM((n_tm, 8, c), f32),
             pltpu.VMEM((positions, 9 * c), bf16),
@@ -285,19 +289,23 @@
             pltpu.VMEM((piece, c), f32),
             pltpu.VMEM((Z_PART, piece, c), f32),
         ]
-        + [dma((n_tm,))] * 6
+        + [dma((n_tm,))] * 8
         + [dma((n_x,))] * 2
         + [dma((Z_PART,))] * 2,
-        compiler_params=pltpu.CompilerParams(collective_id=0, has_side_effects=True),
-        name="norm_down_grad",
+        compiler_params=pltpu.CompilerParams(
+            collective_id=0, has_side_effects=True, vmem_limit_bytes=40 << 20
+        ),
+        name="block",
     )(
-        conv_out,
+        earlier.reshape(frames_dev, cells, c),
+        activations.reshape(frames_dev, cells, c),
+        conv_weight,
         norm_gain.reshape(1, c),
         norm_bias.reshape(1, c),
         down_weight.reshape(9 * c, c),
-        cot,
-    )
-    grad_down = grad[: 9 * own].reshape(9, own, c).transpose(0, 2, 1).reshape(3, 3, c, own)
+        cotangent.reshape(positions, c),
+    )
+    grad_down = grad.transpose(0, 2, 1).reshape(3, 3, c, own)
     return encoded.reshape(cotangent.shape), grad_down
 
 

time: 71.9 us -> 69.4 us (0.965)
  starting transfers between devices: 12.9 us -> 4.58 us
  waiting for transfers between devices: 2.09 us -> 6.42 us
  local copies, waits for them, and re-layouts: 4.37 us -> 6.01 us
    all_to_all x1 -> x0, starting transfers between devices: 8.29 us -> none  [per_device(): lax.all_to_all(cotangent.reshape(positions, c), 'tm', split_axis=0, conca...]
    ppermute x1, waiting for transfers between devices: 0.01 us -> 6.42 us  [passed_along(): return lax.ppermute(shard, axis, pairs)]
    unnamed x5 -> x14, local copies, waits for them, and re-layouts: 3.02 us -> 6.01 us
    all_to_all x1 -> x0, waiting for transfers between devices: 2.09 us -> none  [per_device(): lax.all_to_all(cotangent.reshape(positions, c), 'tm', split_axis=0, conca...]
    slice x1 -> x0, local copies, waits for them, and re-layouts: 0.73 us -> none  [per_device(): grad[:9 * own].reshape(9, own, c).transpose(0, 2, 1).reshape(3, 3, c, own)]
    pallas_call x2 -> x1, Pallas kernels: 51.5 us -> 51.5 us  [per_device(): pl.pallas_call(functools.partial(block_kernel, n_tm, n_dp, height, width,...]
  transfers between devices with their start and end apart: 2 -> 1, of which waited for: 1 -> 1; matrix products, arithmetic and copies ran while one was open for 0% -> 0% of each run, Pallas kernels for 9% -> 0%
where the time goes in v3:
time: 69.4 us; the launch traced here: 69.2 us
  Pallas kernels  51.5 us (74%)
  waiting for transfers between devices  6.42 us (9%)
  local copies, waits for them, and re-layouts  6.01 us (9%)
  starting transfers between devices  4.58 us (7%)
    pallas_call x1, Pallas kernels, per_device(): pl.pallas_call(functools.partial(block_kernel, n_tm, n_dp, height, width,...  51.5 us
    ppermute x1, waiting for transfers between devices, passed_along(): return lax.ppermute(shard, axis, pairs)  6.42 us
    unnamed x14, local copies, waits for them, and re-layouts  6.01 us
    ppermute x1, starting transfers between devices, passed_along(): return lax.ppermute(shard, axis, pairs)  4.58 us
  transfers between devices with their start and end apart: 1, of which 1 were waited for; matrix products, arithmetic and copies ran while one was open for 0% of the time, Pallas kernels for 0%

profile of v3, /device:TPU:1, one launch (start us, length us, event | category | flops | bytes accessed | tf_op | source)
XLA Modules:
  0.0 69.2 jit_solution(3772045923069989665)
XLA Ops:
  0.6 4.6 %collective-permute-start = (bf16[1,2,64,16,128]{4,3,2,1,0:T(8,128)(2,1)}, bf16[1,2,64,16,128]{4,3,2,1,0:T(8,128)(2,1)S(1)}, u32[]{:S(2)}, u32[]{:S(2)}) collective-permute-start(bf16[1,2,64,16,128]{4,3,2,1,0:T(8,128)(2,1)} %param.6), channel_id=1, source_target_pairs={{0,1},{1,2},{2,3},{3,4},{4,5},{5,6},{6,7},{7,8},{8,9},{9,10},{10,1... | collective-permute-start | bytes 1572872 | tf_op jit(solution)/shard_map/ppermute | solution.py:19
  5.2 6.4 %collective-permute-done = bf16[1,2,64,16,128]{4,3,2,1,0:T(8,128)(2,1)S(1)} collective-permute-done((bf16[1,2,64,16,128]{4,3,2,1,0:T(8,128)(2,1)}, bf16[1,2,64,16,128]{4,3,2,1,0:T(8,128)(2,1)S(1)}, u32[]{:S(2)}, u32[]{:S(2)}) %collective-permute-start) | collective-permute-done | bytes 524320 | tf_op jit(solution)/shard_map/ppermute | solution.py:19
  11.6 0.0 copy-start.4
  11.6 0.0 copy-start.5
  11.6 0.7 copy-done.4
  12.3 0.0 copy-done.5
  12.3 0.0 copy-start
  12.3 1.2 %copy-done = bf16[3,3,3,128,128]{4,3,2,1,0:T(8,128)(2,1)S(1)} copy-done((bf16[3,3,3,128,128]{4,3,2,1,0:T(8,128)(2,1)S(1)}, bf16[3,3,3,128,128]{4,3,2,1,0:T(8,128)(2,1)}, u32[]{:S(2)}) %copy-start) | copy-done | bytes 884760
  13.5 0.0 copy-start.1
  13.5 1.0 %copy-done.1 = bf16[1,2,64,16,128]{4,3,2,1,0:T(8,128)(2,1)S(1)} copy-done((bf16[1,2,64,16,128]{4,3,2,1,0:T(8,128)(2,1)S(1)}, bf16[1,2,64,16,128]{4,3,2,1,0:T(8,128)(2,1)}, u32[]{:S(2)}) %copy-start.1) | copy-done | bytes 524312
  14.5 0.0 copy-start.2
  14.5 1.0 %copy-done.2 = bf16[3,3,128,128]{3,2,1,0:T(8,128)(2,1)S(1)} copy-done((bf16[3,3,128,128]{3,2,1,0:T(8,128)(2,1)S(1)}, bf16[3,3,128,128]{3,2,1,0:T(8,128)(2,1)}, u32[]{:S(2)}) %copy-start.2) | copy-done | bytes 294936
  15.5 0.0 copy-start.3
  15.5 0.9 %copy-done.3 = bf16[1,64,1,8,128]{4,3,2,1,0:T(8,128)(2,1)S(1)} copy-done((bf16[1,64,1,8,128]{4,3,2,1,0:T(8,128)(2,1)S(1)}, bf16[1,64,1,8,128]{4,3,2,1,0:T(8,128)(2,1)}, u32[]{:S(2)}) %copy-start.3) | copy-done | bytes 131096
  16.4 51.5 %block.1 = (bf16[512,128]{1,0:T(8,128)(2,1)S(1)}, f32[9,4,128]{2,1,0:T(4,128)S(1)}) custom-call(bf16[2,1024,128]{2,1,0:T(8,128)(2,1)S(1)} %bitcast.13, bf16[2,1024,128]{2,1,0:T(8,128)(2,1)S(1)} %bitcast.12, bf16[3,3,3,128,128]{4,3,2,1,0:T(8,128)(2,1)S(1)} %copy-done, f32[1,128]{1,0:T(1,128)S(1)} %bitcast.18, f32[1,128]{1,0:T(1,128)S(1)} %bitcast.19, ...), custom_call_target="tpu_custom_call" | custom-call | tf_op jit(solution)/shard_map/block/pallas_call | solution.py:265
  67.9 0.7 copy.11
  68.5 0.6 copy.12
Async XLA Ops:
  0.6 11.0 %collective-permute-start = (bf16[1,2,64,16,128]{4,3,2,1,0:T(8,128)(2,1)}, bf16[1,2,64,16,128]{4,3,2,1,0:T(8,128)(2,1)S(1)}, u32[]{:S(2)}, u32[]{:S(2)}) collective-permute-start(bf16[1,2,64,16,128]{4,3,2,1,0:T(8,128)(2,1)} %param.6), channel_id=1, source_target_pairs={{0,1},{1,2},{2,3},{3,4},{4,5},{5,6},{6,7},{7,8},{8,9},{9,10},{10,1... | collective-permute-start | bytes 1572872 | tf_op jit(solution)/shard_map/ppermute | solution.py:19
  11.6 0.7 copy-start.4
  11.6 0.7 copy-start.5
  12.3 1.2 %copy-start = (bf16[3,3,3,128,128]{4,3,2,1,0:T(8,128)(2,1)S(1)}, bf16[3,3,3,128,128]{4,3,2,1,0:T(8,128)(2,1)}, u32[]{:S(2)}) copy-start(bf16[3,3,3,128,128]{4,3,2,1,0:T(8,128)(2,1)} %weight_ref.1) | copy-start | bytes 2654212
  13.5 1.0 %copy-start.1 = (bf16[1,2,64,16,128]{4,3,2,1,0:T(8,128)(2,1)S(1)}, bf16[1,2,64,16,128]{4,3,2,1,0:T(8,128)(2,1)}, u32[]{:S(2)}) copy-start(bf16[1,2,64,16,128]{4,3,2,1,0:T(8,128)(2,1)} %param.6) | copy-start | bytes 1572868
  14.5 1.0 %copy-start.2 = (bf16[3,3,128,128]{3,2,1,0:T(8,128)(2,1)S(1)}, bf16[3,3,128,128]{3,2,1,0:T(8,128)(2,1)}, u32[]{:S(2)}) copy-start(bf16[3,3,128,128]{3,2,1,0:T(8,128)(2,1)} %param.10) | copy-start | bytes 884740
  15.5 0.9 %copy-start.3 = (bf16[1,64,1,8,128]{4,3,2,1,0:T(8,128)(2,1)S(1)}, bf16[1,64,1,8,128]{4,3,2,1,0:T(8,128)(2,1)}, u32[]{:S(2)}) copy-start(bf16[1,64,1,8,128]{4,3,2,1,0:T(8,128)(2,1)} %param.11) | copy-start | bytes 393220
